TPU v7x, 32 devices: a whole 2x2x4 slice. The times are simulated.
32 devices in a mesh: inst: 4 (over y, x), row: 2 (over core), pitch: 4 (over z).
Axes of the slice: x: 2, y: 2, z: 4, core: 2. Of those that a mesh axis runs over, the one named last changes fastest.
Arguments:
- direction: float32 [4, 5, 12288], P('inst', None, ('row', 'pitch')), may hold values from -6 to 6
- time_matrix: float32 [4, 4], replicated, may hold values from -3 to 3
- volume: float32 [12288], P(('row', 'pitch')), may hold values from 0.5 to 2
- diag_jac: float32 [4, 25, 12288], P('inst', None, ('row', 'pitch')), may hold values from -2.5 to 2.5
- face_jac: float32 [4, 50, 24576], P('inst', None, ('row', 'pitch')), may hold values from -1 to 1
- face_left: int32 [24576], P(('row', 'pitch')), may hold values from 0 to 1535
- face_right: int32 [24576], P(('row', 'pitch')), may hold values from 0 to 1535
- bound_jac: float32 [4, 4, 50, 3072], P('inst', None, None, ('row', 'pitch')), may hold values from -1 to 1
- bound_cell: int32 [4, 3072], P(None, ('row', 'pitch')), may hold values from 0 to 1535
- send_cell: int32 [4, 3072], P(None, ('row', 'pitch')), may hold values from 0 to 1535
Outputs:
- product: float32 [4, 5, 12288], P('inst', None, ('row', 'pitch'))
Inputs may be any that keep to these rules, and one draw needn't show every extreme that they name: `face_left`: a cell index local to the face's block of 1536 cells. `face_right`: a cell index local to the face's block of 1536 cells. `bound_cell`: a cell index local to the face's block of 1536 cells. `send_cell`: a cell index local to the supplying block of 1536 cells.
All inputs are finite; a program needn't handle non-finite values.
Results may differ from a plain program's by a relative error of at most 0.000052.
Values sent between devices are 32-bit elements; how exact they have to be, the bound alone decides.
A program may use at most 128 MiB of HBM per device.

v0:
```python
import jax
import jax.numpy as jnp
from jax import lax
from jax.sharding import PartitionSpec as P


def passed_along(block, axis, distance):
    devices = range(lax.axis_size(axis))
    route = [((i - distance) % len(devices), i) for i in devices]
    return lax.ppermute(block, axis, route)


def padded(block, sides, width, periodic):
    for axis, dim in sides:
        count = lax.axis_size(axis)
        forward = [(i, i + 1) for i in range(count - 1)]
        if periodic:
            forward.append((count - 1, 0))
        backward = [(target, source) for source, target in forward]
        low = lax.ppermute(
            lax.slice_in_dim(block, block.shape[dim] - width, None, axis=dim), axis, forward
        )
        high = lax.ppermute(lax.slice_in_dim(block, 0, width, axis=dim), axis, backward)
        block = jnp.concatenate([low, block, high], axis=dim)
    return block


def per_device(
    direction,
    time_matrix,
    volume,
    diag_jac,
    face_jac,
    face_left,
    face_right,
    bound_jac,
    bound_cell,
    send_cell,
):
    high = lax.Precision.HIGHEST
    field = direction[0]
    cells = field.shape[1]
    count = lax.axis_size("inst")
    position = lax.axis_index("inst")
    coef_row = lax.dynamic_slice_in_dim(time_matrix, position, 1, 0)[0]

    def one_turn(turn, carry):
        moving, total = carry
        moving = passed_along(moving, "inst", 1)
        source = (position - turn) % count
        weight = lax.dynamic_slice_in_dim(coef_row, source, 1, 0)[0]
        return (moving, total + weight * moving)

    start_weight = lax.dynamic_slice_in_dim(coef_row, position, 1, 0)[0]
    moving_last, summed = lax.fori_loop(1, count, one_turn, (field, start_weight * field))
    spectral = summed * volume[None, :]
    blocks = diag_jac[0].reshape(5, 5, cells)
    result = spectral + jnp.einsum("abx,bx->ax", blocks, field, precision=high)
    pair = face_jac[0].reshape(2, 5, 5, face_left.shape[0])
    flux = jnp.einsum("abf,bf->af", pair[0], jnp.take(field, face_left, axis=1), precision=high)
    flux = flux + jnp.einsum(
        "abf,bf->af", pair[1], jnp.take(field, face_right, axis=1), precision=high
    )
    result = result.at[:, face_left].add(flux).at[:, face_right].add(-flux)
    outgoing = jnp.stack([jnp.take(field, send_cell[k], axis=1) for k in range(4)])
    pitch_ghost = padded(outgoing[0:2], (("pitch", 0),), 1, True)
    row_ghost = padded(outgoing[2:4], (("row", 0),), 1, False)
    ghosts = jnp.stack([pitch_ghost[0], pitch_ghost[3], row_ghost[0], row_ghost[3]])
    inner = jnp.stack([jnp.take(field, bound_cell[k], axis=1) for k in range(4)])
    bound_count = bound_cell.shape[1]
    bound_pair = bound_jac[0].reshape(4, 2, 5, 5, bound_count)
    bound_flux = jnp.einsum("kabx,kbx->akx", bound_pair[:, 0], inner, precision=high)
    bound_flux = bound_flux + jnp.einsum("kabx,kbx->akx", bound_pair[:, 1], ghosts, precision=high)
    result = result.at[:, bound_cell.reshape(-1)].add(bound_flux.reshape(5, 4 * bound_count))
    return result[None]


def solution(mesh):
    return jax.shard_map(
        per_device,
        mesh=mesh,
        in_specs=(
            P("inst", None, ("row", "pitch")),
            P(),
            P(("row", "pitch")),
            P("inst", None, ("row", "pitch")),
            P("inst", None, ("row", "pitch")),
            P(("row", "pitch")),
            P(("row", "pitch")),
            P("inst", None, None, ("row", "pitch")),
            P(None, ("row", "pitch")),
            P(None, ("row", "pitch")),
        ),
        out_specs=P("inst", None, ("row", "pitch")),
        check_vma=False,
    )
```

profile of v0, /device:TPU:0, one launch (start us, length us, event | category | flops | bytes accessed | tf_op | source)
XLA Modules:
  0.0 186.3 jit_solution(16137494615711352013)
XLA Ops:
  3.9 1.3 collective-permute-start.4
  7.2 4.4 %collective-permute-start.3 = (f32[1,5,384]{1,2,0:T(8,128)}, f32[1,5,384]{1,2,0:T(8,128)}, u32[]{:S(2)}, u32[]{:S(2)}) collective-permute-start(f32[1,5,384]{1,2,0:T(8,128)} %select_bitcast_fusion.1), channel_id=1, source_target_pairs={{0,4},{1,5},{2,6},{3,7},{8,12},{9,13},{10,14},{11,15},{16,20},{17,... | collective-permute-start | bytes 23048 | tf_op jit(solution)/shard_map/ppermute | solution.py:20
  13.5 5.1 %collective-permute-start.2 = (f32[1,5,384]{1,2,0:T(8,128)}, f32[1,5,384]{1,2,0:T(8,128)}, u32[]{:S(2)}, u32[]{:S(2)}) collective-permute-start(f32[1,5,384]{1,2,0:T(8,128)} %select_bitcast_fusion.2), channel_id=1, source_target_pairs={{1,0},{2,1},{3,2},{0,3},{5,4},{6,5},{7,6},{4,7},{9,8},{10,9},{11,1... | collective-permute-start | bytes 23048 | tf_op jit(solution)/shard_map/ppermute | solution.py:23
  22.8 8.3 %gather_fusion = f32[3072,5]{1,0:T(8,128)S(1)} fusion(f32[5,1536]{0,1:T(8,128)S(1)} %bitcast.108, s32[3072]{0:T(1024)S(1)} %get-tuple-element.182), kind=kCustom, calls=%fused_computation.clone | custom fusion | bytes 135168 | tf_op jit(solution)/shard_map/jit(_take)/gather | solution.py:60
  31.1 3.6 %slice_reduce_fusion = (f32[25,3072]{1,0:T(8,128)}, f32[25,3072]{1,0:T(8,128)}) fusion(f32[1,50,3072]{2,0,1:T(1,128)} %param.20), kind=kLoop, calls=%fused_computation.22 | loop fusion | bytes 1228800 | tf_op jit(solution)/shard_map/slice | solution.py:62
  35.7 6.8 %copy.52 = f32[5,5,3072]{0,1,2:T(8,128)} copy(f32[5,5,3072]{2,1,0:T(8,128)S(1)} %squeeze.58) | data formatting | bytes 614400 | tf_op jit(solution)/shard_map/squeeze | solution.py:60
  42.6 10.8 %gather_fusion.1 = f32[3072,5]{1,0:T(8,128)} fusion(f32[5,1536]{0,1:T(8,128)S(1)} %bitcast.109, s32[3072]{0:T(1024)S(1)} %get-tuple-element.181), kind=kCustom, calls=%fused_computation.2.clone | custom fusion | bytes 135168 | tf_op jit(solution)/shard_map/jit(_take)/gather | solution.py:62
  54.4 6.8 %copy.55 = f32[5,5,3072]{0,1,2:T(8,128)} copy(f32[5,5,3072]{2,1,0:T(8,128)S(1)} %squeeze.59) | data formatting | bytes 614400 | tf_op jit(solution)/shard_map/squeeze | solution.py:62
  62.7 1.1 gather_fusion.4
  64.1 1.1 gather_fusion.3
  65.5 1.1 gather_fusion.2
  66.9 1.6 broadcast_select_fusion.1
  68.6 22.7 %fusion.10 = f32[3072,1,5]{2,1,0:T(1,128)S(1)} fusion(f32[5,3072,1]{0,2,1:T(1,128)S(1)} %bitcast.118, f32[5,5,3072]{0,1,2:T(8,128)} %copy.52), kind=kOutput, calls=%fused_computation.85 | convolution fusion | flops 921600 | bytes 430080 | tf_op jit(solution)/shard_map/abf,bf->af/dot_general | solution.py:60
  91.2 1.8 broadcast_select_fusion
  93.1 21.0 %fusion.11 = f32[3072,1,5]{2,1,0:T(1,128)S(1)} fusion(f32[5,3072,1]{0,2,1:T(1,128)S(1)} %bitcast.119, f32[5,5,3072]{0,1,2:T(8,128)S(1)} %bitcast.103), kind=kOutput, calls=%fused_computation.86 | convolution fusion | flops 921600 | bytes 430080 | tf_op jit(solution)/shard_map/abf,bf->af/dot_general | solution.py:61
  114.1 17.3 %while.17 = (s32[]{:T(128)}, f32[5,1536]{1,0:T(8,128)S(1)}, f32[5,1536]{1,0:T(8,128)S(1)}, s32[]{:T(128)}, f32[4]{0:T(128)S(1)}, /*index=5*/s32[]{:T(128)}, s32[]{:T(128)}, s32[]{:T(128)}, s32[]{:T(128)}) while((s32[]{:T(128)}, f32[5,1536]{1,0:T(8,128)S(1)}, f32[5,1536]{1,0:T(8,128)S(1)}, s32[]{:T(128)}, f32[4]{0:T(128)S(1)}, ...), condition=%wide.region_1.2_spmd, body=%wide.region_0.1_spmd.sunk | while | flops 15377 | bytes 276784 | solution.py:55
  114.1 1.5 collective-permute-start
  116.3 2.8 %collective-permute-done = f32[5,1536]{1,0:T(8,128)S(1)} collective-permute-done((f32[5,1536]{1,0:T(8,128)S(1)}, f32[5,1536]{1,0:T(8,128)S(1)}, u32[]{:S(2)}, u32[]{:S(2)}) %collective-permute-start) | collective-permute-done | bytes 30752 | tf_op jit(solution)/shard_map/while/body/eval_jaxpr/ppermute | solution.py:10
  121.2 3.7 %collective-permute-done = f32[5,1536]{1,0:T(8,128)S(1)} collective-permute-done((f32[5,1536]{1,0:T(8,128)S(1)}, f32[5,1536]{1,0:T(8,128)S(1)}, u32[]{:S(2)}, u32[]{:S(2)}) %collective-permute-start) | collective-permute-done | bytes 30752 | tf_op jit(solution)/shard_map/while/body/eval_jaxpr/ppermute | solution.py:10
  126.4 4.3 %collective-permute-done = f32[5,1536]{1,0:T(8,128)S(1)} collective-permute-done((f32[5,1536]{1,0:T(8,128)S(1)}, f32[5,1536]{1,0:T(8,128)S(1)}, u32[]{:S(2)}, u32[]{:S(2)}) %collective-permute-start) | collective-permute-done | bytes 30752 | tf_op jit(solution)/shard_map/while/body/eval_jaxpr/ppermute | solution.py:10
  131.5 1.2 copy.34
  132.7 18.9 %scatter_custom_fusion = f32[5,1536]{0,1:T(8,128)} fusion(f32[5,1536]{0,1:T(8,128)} %copy.34, s32[3072]{0:T(1024)S(1)} %get-tuple-element.183, f32[3072,5]{1,0:T(8,128)S(1)} %bitcast.114, f32[3072,5]{1,0:T(8,128)S(1)} %bitcast.116), kind=kCustom, calls=%fused_computation.18 | custom fusion | flops 30720 | bytes 3176448 | tf_op jit(solution)/shard_map/scatter-add | solution.py:64
  151.6 19.0 %scatter_custom_fusion.1 = f32[5,1536]{0,1:T(8,128)} fusion(f32[5,1536]{0,1:T(8,128)} %scatter_custom_fusion, s32[3072]{0:T(1024)S(1)} %get-tuple-element.180, f32[3072,5]{1,0:T(8,128)S(1)} %bitcast.115, f32[3072,5]{1,0:T(8,128)S(1)} %bitcast.117), kind=kCustom, calls=%fused_computation.14 | custom fusion | flops 46080 | bytes 3176448 | tf_op jit(solution)/shard_map/scatter-add | solution.py:64
  176.4 9.0 %scatter_fusion = f32[5,1536]{0,1:T(8,128)S(1)} fusion(f32[5,1536]{0,1:T(8,128)S(1)} %copy-done, s32[1536]{0:T(1024)S(1)} %fusion.9, f32[1536,5]{1,0:T(8,128)S(1)} %bitcast.121), kind=kCustom, calls=%fused_computation.12 | custom fusion | flops 7680 | bytes 98304 | tf_op jit(solution)/shard_map/scatter-add | solution.py:74
  (111 shorter events, 27.5 us)
Async XLA Ops:
  0.0 20.5 %copy-start.4 = (f32[1,5,1536]{2,0,1:T(1,128)S(1)}, f32[1,5,1536]{2,0,1:T(1,128)}, u32[]{:S(2)}) copy-start(f32[1,5,1536]{2,0,1:T(1,128)} %param.16) | copy-start | bytes 92164
  0.0 20.5 %copy-start.5 = (s32[3072]{0:T(1024)S(1)}, s32[3072]{0:T(1024)}, u32[]{:S(2)}) copy-start(s32[3072]{0:T(1024)} %param.21) | copy-start | bytes 36868
  0.0 20.6 %copy-start.6 = (s32[3072]{0:T(1024)S(1)}, s32[3072]{0:T(1024)}, u32[]{:S(2)}) copy-start(s32[3072]{0:T(1024)} %param.22) | copy-start | bytes 36868
  0.0 20.6 %copy-start.7 = (s32[4,384]{1,0:T(4,128)S(1)}, s32[4,384]{1,0:T(4,128)}, u32[]{:S(2)}) copy-start(s32[4,384]{1,0:T(4,128)} %param.24) | copy-start | bytes 18436
  0.0 20.7 %copy-start.3 = (f32[1,25,1536]{2,0,1:T(1,128)S(1)}, f32[1,25,1536]{2,0,1:T(1,128)}, u32[]{:S(2)}) copy-start(f32[1,25,1536]{2,0,1:T(1,128)} %param.19) | copy-start | bytes 460804
  2.0 19.2 %copy-start.9 = (f32[4,4]{1,0:T(4,128)S(1)}, f32[4,4]{1,0:T(4,128)}, u32[]{:S(2)}) copy-start(f32[4,4]{1,0:T(4,128)} %param.17) | copy-start | bytes 196
  3.9 166.7 %collective-permute-start.4 = (f32[1,5,384]{1,2,0:T(8,128)}, f32[1,5,384]{1,2,0:T(8,128)}, u32[]{:S(2)}, u32[]{:S(2)}) collective-permute-start(f32[1,5,384]{1,2,0:T(8,128)} %select_bitcast_fusion), channel_id=1, source_target_pairs={{4,0},{5,1},{6,2},{7,3},{12,8},{13,9},{14,10},{15,11},{20,16},{21,... | collective-permute-start | bytes 23048 | tf_op jit(solution)/shard_map/ppermute | solution.py:23
  7.2 164.5 %collective-permute-start.3 = (f32[1,5,384]{1,2,0:T(8,128)}, f32[1,5,384]{1,2,0:T(8,128)}, u32[]{:S(2)}, u32[]{:S(2)}) collective-permute-start(f32[1,5,384]{1,2,0:T(8,128)} %select_bitcast_fusion.1), channel_id=1, source_target_pairs={{0,4},{1,5},{2,6},{3,7},{8,12},{9,13},{10,14},{11,15},{16,20},{17,... | collective-permute-start | bytes 23048 | tf_op jit(solution)/shard_map/ppermute | solution.py:20
  13.5 159.2 %collective-permute-start.2 = (f32[1,5,384]{1,2,0:T(8,128)}, f32[1,5,384]{1,2,0:T(8,128)}, u32[]{:S(2)}, u32[]{:S(2)}) collective-permute-start(f32[1,5,384]{1,2,0:T(8,128)} %select_bitcast_fusion.2), channel_id=1, source_target_pairs={{1,0},{2,1},{3,2},{0,3},{5,4},{6,5},{7,6},{4,7},{9,8},{10,9},{11,1... | collective-permute-start | bytes 23048 | tf_op jit(solution)/shard_map/ppermute | solution.py:23
  20.5 153.2 %collective-permute-start.1 = (f32[1,5,384]{1,2,0:T(8,128)}, f32[1,5,384]{1,2,0:T(8,128)}, u32[]{:S(2)}, u32[]{:S(2)}) collective-permute-start(f32[1,5,384]{1,2,0:T(8,128)} %select_bitcast_fusion.3), channel_id=1, source_target_pairs={{0,1},{1,2},{2,3},{3,0},{4,5},{5,6},{6,7},{7,4},{8,9},{9,10},{10,1... | collective-permute-start | bytes 23048 | tf_op jit(solution)/shard_map/ppermute | solution.py:20
  68.5 24.5 %slice-start = ((s8[12582912]{0:T(1024)(128)(4,1)}), s8[4194304]{0:T(1024)(128)(4,1)S(1)}, s32[]{:S(2)}) async-start(s8[12582912]{0:T(1024)(128)(4,1)} %bitcast.102), calls=%async_computation | async-start | bytes 8388608
  68.5 22.7 %copy-start.1 = (f32[3072,5]{1,0:T(8,128)S(1)}, f32[3072,5]{1,0:T(8,128)}, u32[]{:S(2)}) copy-start(f32[3072,5]{1,0:T(8,128)} %gather_fusion.1) | copy-start | bytes 184324
  68.5 24.5 %slice-start.1 = ((s8[12582912]{0:T(1024)(128)(4,1)}), s8[4194304]{0:T(1024)(128)(4,1)S(1)}, s32[]{:S(2)}) async-start(s8[12582912]{0:T(1024)(128)(4,1)} %bitcast.102), calls=%async_computation.1 | async-start | bytes 8388608
  68.5 24.5 %slice-start.2 = ((s8[12582912]{0:T(1024)(128)(4,1)}), s8[4194304]{0:T(1024)(128)(4,1)S(1)}, s32[]{:S(2)}) async-start(s8[12582912]{0:T(1024)(128)(4,1)} %bitcast.102), calls=%async_computation.2 | async-start | bytes 8388608
  114.1 17.3 %copy-start.8 = (f32[1536]{0:T(1024)S(1)}, f32[1536]{0:T(1024)}, u32[]{:S(2)}) copy-start(f32[1536]{0:T(1024)} %param.18) | copy-start | bytes 18436
  114.1 5.0 %collective-permute-start = (f32[5,1536]{1,0:T(8,128)S(1)}, f32[5,1536]{1,0:T(8,128)S(1)}, u32[]{:S(2)}, u32[]{:S(2)}) collective-permute-start(f32[5,1536]{1,0:T(8,128)S(1)} %get-tuple-element.233), channel_id=1, source_target_pairs={{24,0},{0,8},{8,16},{16,24},{25,1},{1,9},{9,17},{17,25},{26,2},{2,... | collective-permute-start | bytes 92168 | tf_op jit(solution)/shard_map/while/body/eval_jaxpr/ppermute | solution.py:10
  119.9 5.0 %collective-permute-start = (f32[5,1536]{1,0:T(8,128)S(1)}, f32[5,1536]{1,0:T(8,128)S(1)}, u32[]{:S(2)}, u32[]{:S(2)}) collective-permute-start(f32[5,1536]{1,0:T(8,128)S(1)} %get-tuple-element.233), channel_id=1, source_target_pairs={{24,0},{0,8},{8,16},{16,24},{25,1},{1,9},{9,17},{17,25},{26,2},{2,... | collective-permute-start | bytes 92168 | tf_op jit(solution)/shard_map/while/body/eval_jaxpr/ppermute | solution.py:10
  125.7 5.0 %collective-permute-start = (f32[5,1536]{1,0:T(8,128)S(1)}, f32[5,1536]{1,0:T(8,128)S(1)}, u32[]{:S(2)}, u32[]{:S(2)}) collective-permute-start(f32[5,1536]{1,0:T(8,128)S(1)} %get-tuple-element.233), channel_id=1, source_target_pairs={{24,0},{0,8},{8,16},{16,24},{25,1},{1,9},{9,17},{17,25},{26,2},{2,... | collective-permute-start | bytes 92168 | tf_op jit(solution)/shard_map/while/body/eval_jaxpr/ppermute | solution.py:10
  151.6 23.2 %copy-start.2 = (f32[1,4,50,384]{3,1,2,0:T(4,128)S(1)}, f32[1,4,50,384]{3,1,2,0:T(4,128)}, u32[]{:S(2)}) copy-start(f32[1,4,50,384]{3,1,2,0:T(4,128)} %param.23) | copy-start | bytes 921604
  175.2 1.1 copy-start
where the time goes:
time: 187 us; the launch traced here: 186 us
  local copies, waits for them, and re-layouts  60.3 us (32%)
  other arithmetic  57.8 us (31%)
  matrix products  43.7 us (23%)
  starting transfers between devices  13 us (7%)
  waiting for transfers between devices  10.9 us (6%)
    scatter-add x2, other arithmetic, per_device(): result = result.at[:, face_left].add(flux).at[:, face_right].add(-flux)  37.9 us
    dot_general x1, matrix products, per_device(): jnp.einsum('abf,bf->af', pair[0], jnp.take(field, face_left, axis=1), pre...  22.7 us
    dot_general x1, matrix products, per_device(): jnp.einsum('abf,bf->af', pair[1], jnp.take(field, face_right, axis=1), pr...  21 us
    ppermute x3, waiting for transfers between devices, passed_along(): return lax.ppermute(block, axis, route)  10.9 us
    gather x1, local copies, waits for them, and re-layouts, per_device(): jnp.take(field, face_right, axis=1)  10.8 us
    scatter-add x1, other arithmetic, per_device(): result.at[:, bound_cell.reshape(-1)]  9.05 us
    gather x1, local copies, waits for them, and re-layouts, per_device(): jnp.take(field, face_left, axis=1)  8.27 us
    squeeze x2, local copies, waits for them, and re-layouts, per_device(): pair[0]  7.88 us
  transfers between devices with their start and end apart: 7, of which 3 were waited for; matrix products, arithmetic and copies ran while one was open for 78% of the time, Pallas kernels for 0%

commit v1 on v0

v1 whole, which is shorter than its diff:
```python
import functools
import jax
import jax.numpy as jnp
from jax import lax
from jax.experimental import pallas as pl
from jax.experimental.pallas import tpu as pltpu
from jax.sharding import PartitionSpec as P

LANE = 128
COMP = 5
TERMS = 2 * COMP
PACK = 16
GROUP = 4
MESH = pl.DeviceIdType.MESH


def gathered(own, cell):
    low = cell & (LANE - 1)
    high = cell >> 7
    chunks = own.shape[1] * GROUP
    masks = [high == h for h in range(chunks)]
    values = []
    for b in range(COMP):
        found = None
        for h in range(chunks):
            row = own[b, h // GROUP, pl.ds(h % GROUP, 1), :]
            part = jnp.take_along_axis(
                jnp.broadcast_to(row, cell.shape), low, axis=1, mode="promise_in_bounds"
            )
            found = part if h == 0 else jnp.where(masks[h], part, found)
        values.append(found)
    return values


def applied(block, base, values):
    result = []
    for a in range(COMP):
        total = None
        for b in range(COMP):
            term = block(base + COMP * a + b) * values[b]
            total = term if total is None else total + term
        result.append(total)
    return result


def two_terms(value):
    first = value.astype(jnp.bfloat16).astype(jnp.float32)
    return first, value - first


def packed_row(row):
    return jnp.broadcast_to(row, (PACK, LANE)).astype(jnp.bfloat16)


def hot_tile(hot, place, cell_row, value):
    low = packed_row((cell_row & (LANE - 1)).astype(jnp.float32))
    for s in range(0, LANE, PACK):
        index = lax.broadcasted_iota(jnp.int32, (PACK, LANE), 0) + s
        index = index.astype(jnp.float32).astype(jnp.bfloat16)
        hot[s : s + PACK, place : place + LANE] = jnp.where(
            index == low, jnp.bfloat16(value), jnp.bfloat16(0)
        )


def chunk_mask(cell_row):
    index = lax.broadcasted_iota(jnp.int32, (PACK, LANE), 0)
    index = index.astype(jnp.float32).astype(jnp.bfloat16)
    return index == packed_row((cell_row >> 7).astype(jnp.float32))


def kernel(
    n_inst,
    n_row,
    n_pitch,
    tm_ref,
    dir_hbm,
    vol_hbm,
    diag_hbm,
    face_hbm,
    left_hbm,
    right_hbm,
    bound_hbm,
    bcell_hbm,
    scell_hbm,
    out_ref,
    own,
    vol_line,
    vol,
    diag,
    face,
    left,
    right,
    bound,
    bcell,
    scell,
    dirs,
    ghost_out,
    ghost_in,
    flux_terms,
    bound_terms,
    rows,
    hot,
    acc,
    local_sem,
    inst_send,
    inst_recv,
    ghost_send,
    ghost_recv,
):
    t = lax.axis_index("inst")
    r = lax.axis_index("row")
    p = lax.axis_index("pitch")
    blocks = own.shape[1]
    chunks = blocks * GROUP
    f_tiles = left.shape[0]
    faces = f_tiles * LANE
    bounds = bcell.shape[1]
    b_tiles = bounds // LANE

    pairs = [
        (dir_hbm, own),
        (scell_hbm, scell),
        (bcell_hbm, bcell),
        (left_hbm, left),
        (right_hbm, right),
        (face_hbm, face),
        (bound_hbm, bound),
        (diag_hbm, diag),
        (vol_hbm, vol_line),
    ]
    copies = [
        pltpu.make_async_copy(a, b, local_sem.at[i]) for i, (a, b) in enumerate(pairs)
    ]
    for c in copies:
        c.start()

    barrier = pltpu.get_barrier_semaphore()

    def greet(**place):
        pl.semaphore_signal(barrier, inc=1, device_id=place, device_id_type=MESH)

    for o in range(1, n_inst):
        greet(inst=lax.rem(t + o, n_inst))
    up = lax.rem(p + 1, n_pitch)
    down = lax.rem(p + n_pitch - 1, n_pitch)
    greet(pitch=up)
    greet(pitch=down)

    @pl.when(r > 0)
    def _():
        greet(row=r - 1)

    @pl.when(r < n_row - 1)
    def _():
        greet(row=r + 1)

    for c in copies[0:3]:
        c.wait()
    inner = []
    for j in range(b_tiles):
        at = slice(j * LANE, (j + 1) * LANE)
        values = gathered(own, jnp.concatenate([scell[:, at], bcell[:, at]], axis=0))
        for b in range(COMP):
            ghost_out[j, pl.ds(b, GROUP, stride=8), :] = values[b][0:GROUP]
        inner.append([v[GROUP : 2 * GROUP] for v in values])

    greeted = 2 + n_inst - 1
    extra = jnp.where(r > 0, 1, 0) + jnp.where(r < n_row - 1, 1, 0)
    pl.semaphore_wait(barrier, greeted + extra)

    def ghost_copy(k, **place):
        opposite = k ^ 1
        return pltpu.make_async_remote_copy(
            src_ref=ghost_out.at[:, 8 * k : 8 * k + 8],
            dst_ref=ghost_in.at[:, 8 * opposite : 8 * opposite + 8],
            send_sem=ghost_send.at[k],
            recv_sem=ghost_recv.at[opposite],
            device_id=place,
            device_id_type=MESH,
        )

    to_down = ghost_copy(0, pitch=down)
    to_up = ghost_copy(1, pitch=up)
    to_down.start()
    to_up.start()

    @pl.when(r > 0)
    def _():
        ghost_copy(2, row=r - 1).start()

    @pl.when(r < n_row - 1)
    def _():
        ghost_copy(3, row=r + 1).start()

    sends = []
    for o in range(1, n_inst):
        c = pltpu.make_async_remote_copy(
            src_ref=dir_hbm,
            dst_ref=dirs.at[o],
            send_sem=inst_send.at[o],
            recv_sem=inst_recv.at[o],
            device_id={"inst": lax.rem(t + o, n_inst)},
            device_id_type=MESH,
        )
        c.start()
        sends.append(c)

    @pl.when(r == 0)
    def _():
        ghost_in[:, 16:24, :] = jnp.zeros((b_tiles, 8, LANE), jnp.float32)

    @pl.when(r == n_row - 1)
    def _():
        ghost_in[:, 24:32, :] = jnp.zeros((b_tiles, 8, LANE), jnp.float32)

    for c in copies[3:9]:
        c.wait()

    def product(start, size):
        return lax.dot_general(
            rows[:, start : start + size],
            hot[:, start : start + size],
            (((1,), (1,)), ((), ())),
            preferred_element_type=jnp.float32,
        )

    total = None
    for g in range(0, f_tiles, 8):
        block = lambda i, g=g: face[i, g : g + 8, :]
        cell_l = left[g : g + 8, :]
        cell_r = right[g : g + 8, :]
        one = applied(block, 0, gathered(own, cell_l))
        two = applied(block, COMP * COMP, gathered(own, cell_r))
        for a in range(COMP):
            first, rest = two_terms(one[a] + two[a])
            flux_terms[a, g : g + 8, :] = first
            flux_terms[COMP + a, g : g + 8, :] = rest
        for s in range(g, g + 8):
            place = 2 * s * LANE
            row_l = left[s : s + 1, :]
            row_r = right[s : s + 1, :]
            hot_tile(hot, place, row_l, 1.0)
            hot_tile(hot, place + LANE, row_r, -1.0)
            mask_l = chunk_mask(row_l)
            mask_r = chunk_mask(row_r)
            for a in range(TERMS):
                value = packed_row(flux_terms[a, s : s + 1, :])
                at = slice(a * PACK, (a + 1) * PACK)
                zero = jnp.bfloat16(0)
                rows[at, place : place + LANE] = jnp.where(mask_l, value, zero)
                rows[at, place + LANE : place + 2 * LANE] = jnp.where(mask_r, value, zero)
        part = product(2 * g * LANE, 16 * LANE)
        total = part if total is None else total + part
    acc[...] = total

    inner_flux = []
    for j in range(b_tiles):
        at = slice(j * LANE, (j + 1) * LANE)
        inner_flux.append(applied(lambda i, at=at: bound[i, :, at], 0, inner[j]))
        for k in range(GROUP):
            hot_tile(hot, 2 * faces + (j * GROUP + k) * LANE, bcell[k : k + 1, at], 1.0)
    for h in range(chunks):
        vol[h // GROUP, pl.ds(h % GROUP, 1), :] = vol_line[
            h * LANE : (h + 1) * LANE
        ].reshape(1, LANE)

    to_down.wait()
    to_up.wait()

    @pl.when(r > 0)
    def _():
        ghost_copy(2, row=r - 1).wait_send()
        half = ghost_in.at[:, 16:24]
        pltpu.make_async_copy(half, half, ghost_recv.at[2]).wait()

    @pl.when(r < n_row - 1)
    def _():
        ghost_copy(3, row=r + 1).wait_send()
        half = ghost_in.at[:, 24:32]
        pltpu.make_async_copy(half, half, ghost_recv.at[3]).wait()

    for j in range(b_tiles):
        at = slice(j * LANE, (j + 1) * LANE)
        outer = [ghost_in[j, pl.ds(b, GROUP, stride=8), :] for b in range(COMP)]
        flux = applied(lambda i, at=at: bound[i, :, at], COMP * COMP, outer)
        for a in range(COMP):
            first, rest = two_terms(inner_flux[j][a] + flux[a])
            bound_terms[a, j] = first
            bound_terms[COMP + a, j] = rest
        for k in range(GROUP):
            place = 2 * faces + (j * GROUP + k) * LANE
            mask = chunk_mask(bcell[k : k + 1, at])
            for a in range(TERMS):
                value = packed_row(bound_terms[a, j, pl.ds(k, 1), :])
                rows[a * PACK : (a + 1) * PACK, place : place + LANE] = jnp.where(
                    mask, value, jnp.bfloat16(0)
                )
    acc[...] = acc[...] + product(2 * faces, 4 * bounds)

    for c in sends:
        c.wait()
    for q in range(blocks):
        mine = [own[b, q] for b in range(COMP)]
        local = applied(lambda i, q=q: diag[i, q], 0, mine)
        for a in range(COMP):
            mixed = tm_ref[t, t] * mine[a]
            for o in range(1, n_inst):
                mixed = mixed + tm_ref[t, lax.rem(t + n_inst - o, n_inst)] * dirs[o, a, q]
            at = a * PACK + q * GROUP
            both = acc[at : at + GROUP, :]
            at = at + COMP * PACK
            both = both + acc[at : at + GROUP, :]
            out_ref[a, q] = mixed * vol[q] + local[a] + both


def per_device(
    direction,
    time_matrix,
    volume,
    diag_jac,
    face_jac,
    face_left,
    face_right,
    bound_jac,
    bound_cell,
    send_cell,
):
    n_inst = lax.axis_size("inst")
    n_row = lax.axis_size("row")
    n_pitch = lax.axis_size("pitch")
    cells = direction.shape[2]
    faces = face_left.shape[0]
    bounds = bound_cell.shape[1]
    blocks = cells // (GROUP * LANE)
    f_tiles = faces // LANE
    b_tiles = bounds // LANE
    width = 2 * faces + 4 * bounds
    f32, i32, bf16 = jnp.float32, jnp.int32, jnp.bfloat16
    cell_view = (blocks, GROUP, LANE)
    hbm = pl.BlockSpec(memory_space=pl.ANY)
    result = pl.pallas_call(
        functools.partial(kernel, n_inst, n_row, n_pitch),
        out_shape=jax.ShapeDtypeStruct((COMP, *cell_view), f32),
        in_specs=[pl.BlockSpec(memory_space=pltpu.SMEM)] + [hbm] * 9,
        out_specs=pl.BlockSpec(memory_space=pltpu.VMEM),
        scratch_shapes=[
            pltpu.VMEM((COMP, *cell_view), f32),
            pltpu.VMEM((cells,), f32),
            pltpu.VMEM(cell_view, f32),
            pltpu.VMEM((25, *cell_view), f32),
            pltpu.VMEM((50, f_tiles, LANE), f32),
            pltpu.VMEM((f_tiles, LANE), i32),
            pltpu.VMEM((f_tiles, LANE), i32),
            pltpu.VMEM((50, 4, bounds), f32),
            pltpu.VMEM((4, bounds), i32),
            pltpu.VMEM((4, bounds), i32),
            pltpu.VMEM((n_inst, COMP, *cell_view), f32),
            pltpu.VMEM((b_tiles, 32, LANE), f32),
            pltpu.VMEM((b_tiles, 32, LANE), f32),
            pltpu.VMEM((TERMS, f_tiles, LANE), f32),
            pltpu.VMEM((TERMS, b_tiles, GROUP, LANE), f32),
            pltpu.VMEM((TERMS * PACK, width), bf16),
            pltpu.VMEM((LANE, width), bf16),
            pltpu.VMEM((TERMS * PACK, LANE), f32),
            pltpu.SemaphoreType.DMA((9,)),
            pltpu.SemaphoreType.DMA((n_inst,)),
            pltpu.SemaphoreType.DMA((n_inst,)),
            pltpu.SemaphoreType.DMA((4,)),
            pltpu.SemaphoreType.DMA((4,)),
        ],
        compiler_params=pltpu.CompilerParams(collective_id=0, has_side_effects=True),
    )(
        time_matrix,
        direction[0].reshape(COMP, *cell_view),
        volume,
        diag_jac[0].reshape(25, *cell_view),
        face_jac[0].reshape(50, f_tiles, LANE),
        face_left.reshape(f_tiles, LANE),
        face_right.reshape(f_tiles, LANE),
        bound_jac[0].transpose(1, 0, 2),
        bound_cell,
        send_cell,
    )
    return result.reshape(1, COMP, cells)


def solution(mesh):
    return jax.shard_map(
        per_device,
        mesh=mesh,
        in_specs=(
            P("inst", None, ("row", "pitch")),
            P(),
            P(("row", "pitch")),
            P("inst", None, ("row", "pitch")),
            P("inst", None, ("row", "pitch")),
            P(("row", "pitch")),
            P(("row", "pitch")),
            P("inst", None, None, ("row", "pitch")),
            P(None, ("row", "pitch")),
            P(None, ("row", "pitch")),
        ),
        out_specs=P("inst", None, ("row", "pitch")),
        check_vma=False,
    )
```

time: 187 us -> 12.9 us (0.07)
  local copies, waits for them, and re-layouts: 60.3 us -> 1.37 us
  other arithmetic: 57.8 us -> 0 us
  matrix products: 43.7 us -> 0 us
  starting transfers between devices: 13 us -> 0 us
  Pallas kernels: 0 us -> 11.4 us
  waiting for transfers between devices: 10.9 us -> 0 us
    scatter-add x3 -> x0, other arithmetic: 47 us -> none  [the longest x2 37.9 us: per_device(): result = result.at[:, face_left].add(flux).at[:, face_right].add(-flux)]
    dot_general x2 -> x0, matrix products: 43.7 us -> none  [the longest x1 22.7 us: per_device(): jnp.einsum('abf,bf->af', pair[0], jnp.take(field, face_left, axis=1), pre...]
    gather x10 -> x0, local copies, waits for them, and re-layouts: 28.1 us -> none  [the longest x1 10.8 us: per_device(): jnp.take(field, face_right, axis=1)]
    squeeze x6 -> x0, local copies, waits for them, and re-layouts: 15.8 us -> none  [the longest x2 7.88 us: per_device(): pair[0]]
    ppermute x7 -> x0, starting transfers between devices: 13 us -> none  [the longest x2 6.37 us: padded(): lax.ppermute(lax.slice_in_dim(block, 0, width, axis=dim), axis, backward)]
    pallas_call x0 -> x1, Pallas kernels: none -> 11.4 us  [per_device(): pl.pallas_call(functools.partial(kernel, n_inst, n_row, n_pitch), out_sha...]
    ppermute x7 -> x0, waiting for transfers between devices: 10.9 us -> none  [the longest x3 10.9 us: passed_along(): return lax.ppermute(block, axis, route)]
    slice x3 -> x0, local copies, waits for them, and re-layouts: 4.46 us -> none  [the longest x1 3.57 us: per_device(): pair[1]]
  transfers between devices with their start and end apart: 7 -> 0, of which waited for: 3 -> 0; matrix products, arithmetic and copies ran while one was open for 78% -> 0% of each run, Pallas kernels for 0% -> 0%
where the time goes in v1:
time: 12.9 us; the launch traced here: 12.7 us
  Pallas kernels  11.4 us (88%)
  local copies, waits for them, and re-layouts  1.37 us (11%)
    pallas_call x1, Pallas kernels, per_device(): pl.pallas_call(functools.partial(kernel, n_inst, n_row, n_pitch), out_sha...  11.4 us
    unnamed x1, local copies, waits for them, and re-layouts  1.37 us

profile of v1, /device:TPU:0, one launch (start us, length us, event | category | flops | bytes accessed | tf_op | source)
XLA Modules:
  0.0 12.7 jit_solution(13190019415925710657)
XLA Ops:
  0.0 11.4 %shard_map.100 = f32[5,3,4,128]{3,2,1,0:T(4,128)} custom-call(f32[4,4]{1,0:T(4,128)} %tm_ref.1, f32[5,3,4,128]{3,2,1,0:T(4,128)} %bitcast.13, f32[1536]{0:T(1024)} %vol_hbm.1, f32[25,3,4,128]{3,2,1,0:T(4,128)} %bitcast.11, f32[50,24,128]{2,1,0:T(8,128)} %bitcast.9, s32[24,128]{1,0:T(8,128)} %bitcast.14, s32[24,128]{1,0:T(8,128)} %bitcast.15, ...), custom_call_target="tpu_custom_call" | custom-call | tf_op jit(solution)/shard_map/pallas_call | solution.py:341
  11.4 1.4 %copy.14 = f32[1,5,1536]{2,0,1:T(1,128)} copy(f32[1,5,1536]{2,0,1:T(1,128)} %bitcast.12) | data formatting | bytes 61440

commit v2 on v1

--- a/solution.py
+++ b/solution.py
@@ -72,7 +72,7 @@
     n_inst,
     n_row,
     n_pitch,
-    tm_ref,
+    tm_hbm,
     dir_hbm,
     vol_hbm,
     diag_hbm,
@@ -83,6 +83,7 @@
     bcell_hbm,
     scell_hbm,
     out_ref,
+    tm_ref,
     own,
     vol_line,
     vol,
@@ -117,6 +118,27 @@
     bounds = bcell.shape[1]
     b_tiles = bounds // LANE
 
+    barrier = pltpu.get_barrier_semaphore()
+
+    def greet(**place):
+        pl.semaphore_signal(barrier, inc=1, device_id=place, device_id_type=MESH)
+
+    up = lax.rem(p + 1, n_pitch)
+    down = lax.rem(p + n_pitch - 1, n_pitch)
+    greet(pitch=up)
+    greet(pitch=down)
+
+    @pl.when(r > 0)
+    def _():
+        greet(row=r - 1)
+
+    @pl.when(r < n_row - 1)
+    def _():
+        greet(row=r + 1)
+
+    for o in range(1, n_inst):
+        greet(inst=lax.rem(t + o, n_inst))
+
     pairs = [
         (dir_hbm, own),
         (scell_hbm, scell),
@@ -127,32 +149,13 @@
         (bound_hbm, bound),
         (diag_hbm, diag),
         (vol_hbm, vol_line),
+        (tm_hbm, tm_ref),
     ]
     copies = [
         pltpu.make_async_copy(a, b, local_sem.at[i]) for i, (a, b) in enumerate(pairs)
     ]
     for c in copies:
         c.start()
-
-    barrier = pltpu.get_barrier_semaphore()
-
-    def greet(**place):
-        pl.semaphore_signal(barrier, inc=1, device_id=place, device_id_type=MESH)
-
-    for o in range(1, n_inst):
-        greet(inst=lax.rem(t + o, n_inst))
-    up = lax.rem(p + 1, n_pitch)
-    down = lax.rem(p + n_pitch - 1, n_pitch)
-    greet(pitch=up)
-    greet(pitch=down)
-
-    @pl.when(r > 0)
-    def _():
-        greet(row=r - 1)
-
-    @pl.when(r < n_row - 1)
-    def _():
-        greet(row=r + 1)
 
     for c in copies[0:3]:
         c.wait()
@@ -171,8 +174,8 @@
     def ghost_copy(k, **place):
         opposite = k ^ 1
         return pltpu.make_async_remote_copy(
-            src_ref=ghost_out.at[:, 8 * k : 8 * k + 8],
-            dst_ref=ghost_in.at[:, 8 * opposite : 8 * opposite + 8],
+            src_ref=ghost_out.at[:, 8 * k : 8 * k + COMP],
+            dst_ref=ghost_in.at[:, 8 * opposite : 8 * opposite + COMP],
             send_sem=ghost_send.at[k],
             recv_sem=ghost_recv.at[opposite],
             device_id=place,
@@ -213,7 +216,7 @@
     def _():
         ghost_in[:, 24:32, :] = jnp.zeros((b_tiles, 8, LANE), jnp.float32)
 
-    for c in copies[3:9]:
+    for c in copies[3:10]:
         c.wait()
 
     def product(start, size):
@@ -253,49 +256,20 @@
         total = part if total is None else total + part
     acc[...] = total
 
+    def boundary_place(j, k):
+        pair = 1 - k // 2
+        return 2 * faces + 2 * pair * bounds + (2 * j + k % 2) * LANE
+
     inner_flux = []
     for j in range(b_tiles):
         at = slice(j * LANE, (j + 1) * LANE)
         inner_flux.append(applied(lambda i, at=at: bound[i, :, at], 0, inner[j]))
         for k in range(GROUP):
-            hot_tile(hot, 2 * faces + (j * GROUP + k) * LANE, bcell[k : k + 1, at], 1.0)
+            hot_tile(hot, boundary_place(j, k), bcell[k : k + 1, at], 1.0)
     for h in range(chunks):
         vol[h // GROUP, pl.ds(h % GROUP, 1), :] = vol_line[
             h * LANE : (h + 1) * LANE
         ].reshape(1, LANE)
-
-    to_down.wait()
-    to_up.wait()
-
-    @pl.when(r > 0)
-    def _():
-        ghost_copy(2, row=r - 1).wait_send()
-        half = ghost_in.at[:, 16:24]
-        pltpu.make_async_copy(half, half, ghost_recv.at[2]).wait()
-
-    @pl.when(r < n_row - 1)
-    def _():
-        ghost_copy(3, row=r + 1).wait_send()
-        half = ghost_in.at[:, 24:32]
-        pltpu.make_async_copy(half, half, ghost_recv.at[3]).wait()
-
-    for j in range(b_tiles):
-        at = slice(j * LANE, (j + 1) * LANE)
-        outer = [ghost_in[j, pl.ds(b, GROUP, stride=8), :] for b in range(COMP)]
-        flux = applied(lambda i, at=at: bound[i, :, at], COMP * COMP, outer)
-        for a in range(COMP):
-            first, rest = two_terms(inner_flux[j][a] + flux[a])
-            bound_terms[a, j] = first
-            bound_terms[COMP + a, j] = rest
-        for k in range(GROUP):
-            place = 2 * faces + (j * GROUP + k) * LANE
-            mask = chunk_mask(bcell[k : k + 1, at])
-            for a in range(TERMS):
-                value = packed_row(bound_terms[a, j, pl.ds(k, 1), :])
-                rows[a * PACK : (a + 1) * PACK, place : place + LANE] = jnp.where(
-                    mask, value, jnp.bfloat16(0)
-                )
-    acc[...] = acc[...] + product(2 * faces, 4 * bounds)
 
     for c in sends:
         c.wait()
@@ -306,11 +280,54 @@
             mixed = tm_ref[t, t] * mine[a]
             for o in range(1, n_inst):
                 mixed = mixed + tm_ref[t, lax.rem(t + n_inst - o, n_inst)] * dirs[o, a, q]
+            out_ref[a, q] = mixed * vol[q] + local[a]
+
+    def boundary(start):
+        for j in range(b_tiles):
+            at = slice(j * LANE, (j + 1) * LANE)
+            outer = [
+                ghost_in[j, pl.ds(8 * start + b, 2, stride=8), :] for b in range(COMP)
+            ]
+            block = lambda i, at=at: bound[i, start : start + 2, at]
+            flux = applied(block, COMP * COMP, outer)
+            for a in range(COMP):
+                first, rest = two_terms(inner_flux[j][a][start : start + 2] + flux[a])
+                bound_terms[a, j, start : start + 2, :] = first
+                bound_terms[COMP + a, j, start : start + 2, :] = rest
+            for k in range(start, start + 2):
+                place = boundary_place(j, k)
+                mask = chunk_mask(bcell[k : k + 1, at])
+                for a in range(TERMS):
+                    value = packed_row(bound_terms[a, j, pl.ds(k, 1), :])
+                    rows[a * PACK : (a + 1) * PACK, place : place + LANE] = jnp.where(
+                        mask, value, jnp.bfloat16(0)
+                    )
+
+    @pl.when(r > 0)
+    def _():
+        ghost_copy(2, row=r - 1).wait_send()
+        half = ghost_in.at[:, 16 : 16 + COMP]
+        pltpu.make_async_copy(half, half, ghost_recv.at[2]).wait()
+
+    @pl.when(r < n_row - 1)
+    def _():
+        ghost_copy(3, row=r + 1).wait_send()
+        half = ghost_in.at[:, 24 : 24 + COMP]
+        pltpu.make_async_copy(half, half, ghost_recv.at[3]).wait()
+
+    boundary(2)
+    acc[...] = acc[...] + product(2 * faces, 2 * bounds)
+
+    to_down.wait()
+    to_up.wait()
+    boundary(0)
+    acc[...] = acc[...] + product(2 * faces + 2 * bounds, 2 * bounds)
+    for q in range(blocks):
+        for a in range(COMP):
             at = a * PACK + q * GROUP
             both = acc[at : at + GROUP, :]
             at = at + COMP * PACK
-            both = both + acc[at : at + GROUP, :]
-            out_ref[a, q] = mixed * vol[q] + local[a] + both
+            out_ref[a, q] = out_ref[a, q] + (both + acc[at : at + GROUP, :])
 
 
 def per_device(
@@ -340,10 +357,11 @@
     hbm = pl.BlockSpec(memory_space=pl.ANY)
     result = pl.pallas_call(
         functools.partial(kernel, n_inst, n_row, n_pitch),
-        out_shape=jax.ShapeDtypeStruct((COMP, *cell_view), f32),
-        in_specs=[pl.BlockSpec(memory_space=pltpu.SMEM)] + [hbm] * 9,
+        out_shape=pltpu.VMEM((COMP, *cell_view), f32),
+        in_specs=[hbm] * 10,
         out_specs=pl.BlockSpec(memory_space=pltpu.VMEM),
         scratch_shapes=[
+            pltpu.SMEM((n_inst, n_inst), f32),
             pltpu.VMEM((COMP, *cell_view), f32),
             pltpu.VMEM((cells,), f32),
             pltpu.VMEM(cell_view, f32),
@@ -362,7 +380,7 @@
             pltpu.VMEM((TERMS * PACK, width), bf16),
             pltpu.VMEM((LANE, width), bf16),
             pltpu.VMEM((TERMS * PACK, LANE), f32),
-            pltpu.SemaphoreType.DMA((9,)),
+            pltpu.SemaphoreType.DMA((10,)),
             pltpu.SemaphoreType.DMA((n_inst,)),
             pltpu.SemaphoreType.DMA((n_inst,)),
             pltpu.SemaphoreType.DMA((4,)),

time: 12.9 us -> 11.1 us (0.86)
  Pallas kernels: 11.4 us -> 10.4 us
  local copies, waits for them, and re-layouts: 1.37 us -> 0.61 us
    pallas_call x1, Pallas kernels: 11.4 us -> 10.4 us  [per_device(): pl.pallas_call(functools.partial(kernel, n_inst, n_row, n_pitch), out_sha...]
    unnamed x1, local copies, waits for them, and re-layouts: 1.37 us -> 0.61 us
where the time goes in v2:
time: 11.1 us; the launch traced here: 11 us
  Pallas kernels  10.4 us (94%)
  local copies, waits for them, and re-layouts  0.61 us (5%)
    pallas_call x1, Pallas kernels, per_device(): pl.pallas_call(functools.partial(kernel, n_inst, n_row, n_pitch), out_sha...  10.4 us
    unnamed x1, local copies, waits for them, and re-layouts  0.61 us

profile of v2, /device:TPU:0, one launch (start us, length us, event | category | flops | bytes accessed | tf_op | source)
XLA Modules:
  0.0 11.0 jit_solution(18255157467903904558)
XLA Ops:
  0.0 10.4 %shard_map.100 = f32[5,3,4,128]{3,2,1,0:T(4,128)S(1)} custom-call(f32[4,4]{1,0:T(4,128)} %tm_hbm.1, f32[5,3,4,128]{3,2,1,0:T(4,128)} %bitcast.13, f32[1536]{0:T(1024)} %vol_hbm.1, f32[25,3,4,128]{3,2,1,0:T(4,128)} %bitcast.12, f32[50,24,128]{2,1,0:T(8,128)} %bitcast.10, s32[24,128]{1,0:T(8,128)} %bitcast.14, s32[24,128]{1,0:T(8,128)} %bitcast.15, ...), custom_call_target="tpu_custom_call" | custom-call | tf_op jit(solution)/shard_map/pallas_call | solution.py:358
  10.4 0.6 %copy.14 = f32[1,5,1536]{2,0,1:T(1,128)} copy(f32[1,5,1536]{2,0,1:T(1,128)S(1)} %bitcast.9) | data formatting | bytes 61440

commit v3 on v2

--- a/solution.py
+++ b/solution.py
@@ -271,16 +271,10 @@
             h * LANE : (h + 1) * LANE
         ].reshape(1, LANE)
 
-    for c in sends:
-        c.wait()
     for q in range(blocks):
-        mine = [own[b, q] for b in range(COMP)]
-        local = applied(lambda i, q=q: diag[i, q], 0, mine)
+        local = applied(lambda i, q=q: diag[i, q], 0, [own[b, q] for b in range(COMP)])
         for a in range(COMP):
-            mixed = tm_ref[t, t] * mine[a]
-            for o in range(1, n_inst):
-                mixed = mixed + tm_ref[t, lax.rem(t + n_inst - o, n_inst)] * dirs[o, a, q]
-            out_ref[a, q] = mixed * vol[q] + local[a]
+            out_ref[a, q] = local[a] + (tm_ref[t, t] * own[a, q]) * vol[q]
 
     def boundary(start):
         for j in range(b_tiles):
@@ -318,10 +312,25 @@
     boundary(2)
     acc[...] = acc[...] + product(2 * faces, 2 * bounds)
 
+    for c in sends:
+        c.wait()
+    weights = [tm_ref[t, lax.rem(t + n_inst - o, n_inst)] for o in range(1, n_inst)]
+    for q in range(blocks):
+        for a in range(COMP):
+            mixed = None
+            for o in range(1, n_inst):
+                term = weights[o - 1] * dirs[o, a, q]
+                mixed = term if mixed is None else mixed + term
+            at = a * PACK + q * GROUP
+            both = acc[at : at + GROUP, :]
+            at = at + COMP * PACK
+            both = both + acc[at : at + GROUP, :]
+            out_ref[a, q] = out_ref[a, q] + mixed * vol[q] + both
+
     to_down.wait()
     to_up.wait()
     boundary(0)
-    acc[...] = acc[...] + product(2 * faces + 2 * bounds, 2 * bounds)
+    acc[...] = product(2 * faces + 2 * bounds, 2 * bounds)
     for q in range(blocks):
         for a in range(COMP):
             at = a * PACK + q * GROUP

time: 11.1 us -> 10.9 us (0.982)
  Pallas kernels: 10.4 us -> 10.2 us
    pallas_call x1, Pallas kernels: 10.4 us -> 10.2 us  [per_device(): pl.pallas_call(functools.partial(kernel, n_inst, n_row, n_pitch), out_sha...]
where the time goes in v3:
time: 10.9 us; the launch traced here: 10.8 us
  Pallas kernels  10.2 us (94%)
  local copies, waits for them, and re-layouts  0.61 us (6%)
    pallas_call x1, Pallas kernels, per_device(): pl.pallas_call(functools.partial(kernel, n_inst, n_row, n_pitch), out_sha...  10.2 us
    unnamed x1, local copies, waits for them, and re-layouts  0.61 us

profile of v3, /device:TPU:0, one launch (start us, length us, event | category | flops | bytes accessed | tf_op | source)
XLA Modules:
  0.0 10.8 jit_solution(3022985896854112827)
XLA Ops:
  0.0 10.2 %shard_map.100 = f32[5,3,4,128]{3,2,1,0:T(4,128)S(1)} custom-call(f32[4,4]{1,0:T(4,128)} %tm_hbm.1, f32[5,3,4,128]{3,2,1,0:T(4,128)} %bitcast.13, f32[1536]{0:T(1024)} %vol_hbm.1, f32[25,3,4,128]{3,2,1,0:T(4,128)} %bitcast.12, f32[50,24,128]{2,1,0:T(8,128)} %bitcast.10, s32[24,128]{1,0:T(8,128)} %bitcast.14, s32[24,128]{1,0:T(8,128)} %bitcast.15, ...), custom_call_target="tpu_custom_call" | custom-call | tf_op jit(solution)/shard_map/pallas_call | solution.py:367
  10.2 0.6 %copy.14 = f32[1,5,1536]{2,0,1:T(1,128)} copy(f32[1,5,1536]{2,0,1:T(1,128)S(1)} %bitcast.9) | data formatting | bytes 61440

commit v4 on v3

--- a/solution.py
+++ b/solution.py
@@ -198,7 +198,7 @@
     sends = []
     for o in range(1, n_inst):
         c = pltpu.make_async_remote_copy(
-            src_ref=dir_hbm,
+            src_ref=own,
             dst_ref=dirs.at[o],
             send_sem=inst_send.at[o],
             recv_sem=inst_recv.at[o],

time: 10.9 us -> 10.7 us (0.982)
  Pallas kernels: 10.2 us -> 9.97 us
    pallas_call x1, Pallas kernels: 10.2 us -> 9.97 us  [per_device(): pl.pallas_call(functools.partial(kernel, n_inst, n_row, n_pitch), out_sha...]
where the time goes in v4:
time: 10.7 us; the launch traced here: 10.6 us
  Pallas kernels  9.97 us (93%)
  local copies, waits for them, and re-layouts  0.61 us (6%)
    pallas_call x1, Pallas kernels, per_device(): pl.pallas_call(functools.partial(kernel, n_inst, n_row, n_pitch), out_sha...  9.97 us
    unnamed x1, local copies, waits for them, and re-layouts  0.61 us

profile of v4, /device:TPU:0, one launch (start us, length us, event | category | flops | bytes accessed | tf_op | source)
XLA Modules:
  0.0 10.6 jit_solution(12329330197145887847)
XLA Ops:
  0.0 10.0 %shard_map.100 = f32[5,3,4,128]{3,2,1,0:T(4,128)S(1)} custom-call(f32[4,4]{1,0:T(4,128)} %tm_hbm.1, f32[5,3,4,128]{3,2,1,0:T(4,128)} %bitcast.13, f32[1536]{0:T(1024)} %vol_hbm.1, f32[25,3,4,128]{3,2,1,0:T(4,128)} %bitcast.12, f32[50,24,128]{2,1,0:T(8,128)} %bitcast.10, s32[24,128]{1,0:T(8,128)} %bitcast.14, s32[24,128]{1,0:T(8,128)} %bitcast.15, ...), custom_call_target="tpu_custom_call" | custom-call | tf_op jit(solution)/shard_map/pallas_call | solution.py:367
  10.0 0.6 %copy.14 = f32[1,5,1536]{2,0,1:T(1,128)} copy(f32[1,5,1536]{2,0,1:T(1,128)S(1)} %bitcast.9) | data formatting | bytes 61440
